TPU v7x, 32 devices: a whole 2x2x4 slice. The times are simulated.
32 devices in a mesh: dp: 4 (over x, core), fsdp: 8 (over z, y).
Axes of the slice: x: 2, y: 2, z: 4, core: 2. Of those that a mesh axis runs over, the one named last changes fastest.
Arguments:
- tokens: bfloat16 [4, 1024, 768], P('dp', 'fsdp'), may hold values from -6 to 6
- ln1_gain: bfloat16 [768], P('fsdp'), may hold values from 0.099609375 to 1.8984375
- ln1_bias: bfloat16 [768], P('fsdp'), may hold values from -1.75 to 1.75
- ln2_gain: bfloat16 [768], P('fsdp'), may hold values from 0.099609375 to 1.8984375
- ln2_bias: bfloat16 [768], P('fsdp'), may hold values from -1.75 to 1.75
- qkv_weight: bfloat16 [768, 2304], P('fsdp'), may hold values from -0.21875 to 0.21875
- qkv_bias: bfloat16 [2304], P('fsdp'), may hold values from -3 to 3
- out_weight: bfloat16 [768, 768], P('fsdp'), may hold values from -1.75 to 1.75
- out_bias: bfloat16 [768], P('fsdp'), may hold values from -3 to 3
- up_weight: bfloat16 [768, 3072], P('fsdp'), may hold values from -0.21875 to 0.21875
- up_bias: bfloat16 [3072], P('fsdp'), may hold values from -3 to 3
- down_weight: bfloat16 [3072, 768], P('fsdp'), may hold values from -0.109375 to 0.109375
- down_bias: bfloat16 [768], P('fsdp'), may hold values from -3 to 3
- cotangent: bfloat16 [4, 1024, 768], P('dp', 'fsdp'), may hold values from -6 to 6
Outputs:
- layer_output: bfloat16 [4, 1024, 768], P('dp', 'fsdp')
- input_grad: float32 [4, 1024, 768], P('dp', 'fsdp')
- grad_ln1_gain: float32 [768], P('fsdp')
- grad_ln1_bias: float32 [768], P('fsdp')
- grad_ln2_gain: float32 [768], P('fsdp')
- grad_ln2_bias: float32 [768], P('fsdp')
- grad_qkv_weight: float32 [768, 2304], P('fsdp')
- grad_qkv_bias: float32 [2304], P('fsdp')
- grad_out_weight: float32 [768, 768], P('fsdp')
- grad_out_bias: float32 [768], P('fsdp')
- grad_up_weight: float32 [768, 3072], P('fsdp')
- grad_up_bias: float32 [3072], P('fsdp')
- grad_down_weight: float32 [3072, 768], P('fsdp')
- grad_down_bias: float32 [768], P('fsdp')
All inputs are finite; a program needn't handle non-finite values.
Results may differ from a plain program's by a relative error of at most 0.018.
Values may be sent and summed in bfloat16 or wider, within the bound.
A program may use at most 128 MiB of HBM per device.

v0:
```python
import math
import jax
import jax.numpy as jnp
from jax import lax
from jax.sharding import PartitionSpec as P

HEADS = 12
HEAD = 64
ROT = 16
epsilon = 1e-05
inv_root_two = 1.0 / math.sqrt(2.0)
inv_root_twopi = 1.0 / math.sqrt(2.0 * math.pi)
bf16 = jnp.bfloat16
f32 = jnp.float32


def rotary(tensor, cosine, sine, direction):
    half = ROT // 2
    first = tensor[..., :half]
    second = tensor[..., half:ROT]
    return jnp.concatenate(
        [
            first * cosine - direction * second * sine,
            second * cosine + direction * first * sine,
            tensor[..., ROT:],
        ],
        axis=-1,
    )


def dot(a, b, dims):
    return lax.dot_general(a, b, ((dims[0], dims[1]), ((), ())), preferred_element_type=f32)


NN = ((1,), (0,))
NT = ((1,), (1,))
TN = ((0,), (0,))


def gather_rows(arrays):
    return [lax.all_gather(a, "fsdp", axis=0, tiled=True) for a in arrays]


def scatter_rows(a):
    F = lax.axis_size("fsdp")
    got = lax.all_to_all(a, "fsdp", 0, 0, tiled=True)
    return jnp.sum(got.reshape((F, a.shape[0] // F) + a.shape[1:]).astype(f32), axis=0)


def spread_weights(blocks):
    return lax.all_to_all(blocks, "fsdp", 0, 0, tiled=True)


def return_grads(blocks, own):
    n = lax.axis_size("dp")
    F, W, C = blocks.shape
    R, D = own.shape
    parts = jnp.swapaxes(blocks.reshape(F, n, W // n, C), 0, 1).reshape(n, F * (W // n), C)
    own_parts = own.reshape(n, R // n, D)
    if C == D:
        both = jnp.concatenate([parts, own_parts], axis=1)
        both = jnp.sum(lax.all_to_all(both, "dp", 0, 0, tiled=True).astype(f32), axis=0)
        part, own_part = (both[: F * (W // n)].astype(bf16), both[F * (W // n) :].astype(bf16))
    else:
        part = jnp.sum(lax.all_to_all(parts, "dp", 0, 0, tiled=True).astype(f32), axis=0)
        own_part = jnp.sum(lax.all_to_all(own_parts, "dp", 0, 0, tiled=True).astype(f32), axis=0)
        part, own_part = (part.astype(bf16), own_part.astype(bf16))
    part = lax.all_to_all(part, "fsdp", 0, 0, tiled=True)
    if C == D:
        whole = lax.all_gather(jnp.concatenate([part, own_part], axis=0), "dp", axis=0)
        part_all, own_all = (whole[:, : F * (W // n)], whole[:, F * (W // n) :])
    else:
        part_all = lax.all_gather(part, "dp", axis=0)
        own_all = lax.all_gather(own_part, "dp", axis=0)
    part_all = jnp.swapaxes(part_all.reshape(n, F, W // n, C), 0, 1).reshape(F, W, C)
    return (part_all, own_all.reshape(R, D))


def body(
    tokens,
    ln1_gain,
    ln1_bias,
    ln2_gain,
    ln2_bias,
    qkv_weight,
    qkv_bias,
    out_weight,
    out_bias,
    up_weight,
    up_bias,
    down_weight,
    down_bias,
    cotangent,
):
    rank = lax.axis_index("fsdp")
    F = lax.axis_size("fsdp")
    rows, D = tokens.shape[1:]
    W = D // F
    FFW = down_weight.shape[0]
    NH = max((-(-(g * W % HEAD + W) // HEAD) for g in range(F)))
    WIN = NH * HEAD
    starts = [min(g * W // HEAD, HEADS - NH) * HEAD for g in range(F)]
    start = jnp.minimum(rank * W // HEAD, HEADS - NH) * HEAD
    off = rank * W - start
    S = rows * F
    qkv3 = qkv_weight.reshape(W, 3, D)
    blocks = jnp.stack(
        [
            jnp.concatenate(
                [
                    qkv3[:, 0, s : s + WIN],
                    qkv3[:, 1, s : s + WIN],
                    qkv3[:, 2, s : s + WIN],
                    up_weight[:, g * FFW : (g + 1) * FFW],
                ],
                axis=1,
            )
            for g, s in enumerate(starts)
        ]
    )
    smalls = jnp.concatenate(
        [ln1_gain, ln1_bias, ln2_gain, ln2_bias, out_bias, down_bias, qkv_bias]
    )
    extra = -(-smalls.shape[0] // (16 * D)) * 16
    smalls = jnp.concatenate([smalls, jnp.zeros(extra * D - smalls.shape[0], bf16)])
    (both_all,) = gather_rows([jnp.concatenate([tokens[0], smalls.reshape(extra, D)], axis=0)])
    both_all = both_all.reshape(F, rows + extra, D)
    x_low = both_all[:, :rows].reshape(S, D)
    small_all = both_all[:, rows:].reshape(F, extra * D)
    wall = spread_weights(blocks).reshape(D, 3 * WIN + FFW)
    w_qkv = wall[:, : 3 * WIN]
    w_up = wall[:, 3 * WIN :]
    up_ring = [(i, (i + 1) % F) for i in range(F)]
    down_ring = [(i, (i - 1) % F) for i in range(F)]
    out_prev = lax.ppermute(out_weight, "fsdp", up_ring)
    out_next = lax.ppermute(out_weight, "fsdp", down_ring)
    (grad_out,) = gather_rows([cotangent[0]])
    out_three = jnp.concatenate([out_prev, out_weight, out_next, jnp.zeros((WIN, D), bf16)], axis=0)
    w_out_win = lax.dynamic_slice_in_dim(out_three, W - off, WIN, 0)
    win_col = jnp.arange(WIN, dtype=jnp.int32)
    mine = (win_col >= off) & (win_col < off + W)
    small_all = small_all.astype(f32)
    gain_one, bias_one, gain_two, bias_two, b_out, b_down = [
        small_all[:, i * W : (i + 1) * W].reshape(D) for i in range(6)
    ]
    b_qkv = small_all[:, 6 * W : 9 * W].reshape(3, D)
    b_qkv = lax.dynamic_slice_in_dim(b_qkv, start, WIN, 1).reshape(3 * WIN)
    b_up = up_bias.astype(f32)
    x = x_low.astype(f32)
    center = x - jnp.mean(x, axis=-1, keepdims=True)
    inverse = lax.rsqrt(jnp.mean(center * center, axis=-1, keepdims=True) + epsilon)
    normed = center * inverse
    first_low = (normed * gain_one + bias_one).astype(bf16)
    second_low = (normed * gain_two + bias_two).astype(bf16)
    places = jnp.arange(S, dtype=f32)
    half = ROT // 2
    freq = 10000.0 ** (-(jnp.arange(half, dtype=f32) * 2.0) / ROT)
    angle = places[:, None] * freq[None, :]
    cosine = jnp.cos(angle)[:, None, :]
    sine = jnp.sin(angle)[:, None, :]
    proj = dot(first_low, w_qkv, NN) + b_qkv
    queries = (rotary(proj[:, :WIN].reshape(S, NH, HEAD), cosine, sine, 1.0) * 0.125).astype(bf16)
    keys = rotary(proj[:, WIN : 2 * WIN].reshape(S, NH, HEAD), cosine, sine, 1.0).astype(bf16)
    vals = proj[:, 2 * WIN :].astype(bf16).reshape(S, NH, HEAD)
    q_place = jnp.arange(S, dtype=jnp.int32)
    visible = (q_place[None, :] <= q_place[:, None])[None]
    scores = jnp.einsum("qhd,khd->hqk", queries, keys, preferred_element_type=f32)
    masked = jnp.where(visible, scores, -1e30)
    top = jnp.max(masked, axis=-1, keepdims=True)
    lse = top + jnp.log(jnp.sum(jnp.exp(masked - top), axis=-1, keepdims=True))
    probs = jnp.exp(masked - lse)
    probs_low = probs.astype(bf16)
    attended = jnp.einsum("hqk,khd->qhd", probs_low, vals, preferred_element_type=f32)
    att_low = jnp.where(mine, attended.reshape(S, WIN), 0.0).astype(bf16)
    hidden_pre = dot(second_low, w_up, NN) + b_up
    cdf = 0.5 * (1.0 + lax.erf(hidden_pre * inv_root_two))
    hidden_low = (hidden_pre * cdf).astype(bf16)
    part = dot(att_low, w_out_win, NN) + dot(hidden_low, down_weight, NN)
    branch = scatter_rows(part.astype(bf16))
    grad_hidden = dot(grad_out, down_weight, NT)
    slope = cdf + hidden_pre * jnp.exp(-0.5 * hidden_pre * hidden_pre) * inv_root_twopi
    grad_pre = (grad_hidden * slope).astype(bf16)
    grad_w_down = dot(hidden_low, grad_out, TN)
    grad_w_out_win = dot(att_low, grad_out, TN)
    grad_w_out = lax.dynamic_slice_in_dim(grad_w_out_win, off, W, 0)
    bias_total = jnp.sum(grad_out.astype(f32), axis=0)
    grad_b_up = jnp.sum(grad_pre.astype(f32), axis=0)
    grad_att = dot(grad_out, w_out_win, NT).astype(bf16).reshape(S, NH, HEAD)
    delta = jnp.transpose(jnp.sum(grad_att.astype(f32) * attended, axis=-1))[:, :, None]
    grad_probs = jnp.einsum("qhd,khd->hqk", grad_att, vals, preferred_element_type=f32)
    grad_scores = (probs * (grad_probs - delta)).astype(bf16)
    grad_q = jnp.einsum("hqk,khd->qhd", grad_scores, keys, preferred_element_type=f32)
    grad_k = jnp.einsum("hqk,qhd->khd", grad_scores, queries, preferred_element_type=f32)
    grad_v = jnp.einsum("hqk,qhd->khd", probs_low, grad_att, preferred_element_type=f32)
    grad_proj = jnp.stack(
        [
            rotary(grad_q * 0.125, cosine, sine, -1.0).reshape(S, WIN),
            rotary(grad_k, cosine, sine, -1.0).reshape(S, WIN),
            grad_v.reshape(S, WIN),
        ],
        axis=1,
    )
    grad_proj = jnp.where(mine, grad_proj, 0.0).astype(bf16).reshape(S, 3 * WIN)
    grad_w_qkv = dot(first_low, grad_proj, TN)
    grad_w_up = dot(second_low, grad_pre, TN)
    grad_b_qkv = jnp.sum(grad_proj.astype(f32), axis=0).reshape(3, WIN)
    grad_first = dot(grad_proj, w_qkv, NT)
    grad_second = dot(grad_pre, w_up, NT)
    vectors = [
        jnp.sum(grad_first * normed, axis=0),
        jnp.sum(grad_first, axis=0),
        jnp.sum(grad_second * normed, axis=0),
        jnp.sum(grad_second, axis=0),
    ]
    mixed = grad_first * gain_one + grad_second * gain_two
    b_full = lax.dynamic_update_slice_in_dim(jnp.zeros((3, D), f32), grad_b_qkv, start, 1)
    small_part = jnp.concatenate(
        [v.reshape(F, W) for v in vectors] + [b_full.reshape(F, 3 * W)], axis=1
    )
    mixed_mine = scatter_rows(mixed.astype(bf16))
    small_mine = scatter_rows(small_part)[0]
    own_small = jnp.concatenate(
        [small_mine, lax.dynamic_slice_in_dim(bias_total, rank * W, W, 0), grad_b_up]
    )
    pad = 8 * lax.axis_size("dp")
    own_rows = -(-(W + FFW + -(-own_small.shape[0] // D)) // pad) * pad
    n_small = own_rows - W - FFW
    own_small = jnp.concatenate([own_small, jnp.zeros(n_small * D - own_small.shape[0], f32)])
    grad_blocks = jnp.concatenate([grad_w_qkv, grad_w_up], axis=1).astype(bf16)
    grad_blocks = grad_blocks.reshape(F, W, 3 * WIN + FFW)
    own = jnp.concatenate([grad_w_out, grad_w_down, own_small.reshape(n_small, D)], axis=0).astype(
        bf16
    )
    returned, own = return_grads(grad_blocks, own)
    returned = returned.astype(f32)
    own = own.astype(f32)
    own_small = own[W + FFW :].reshape(n_small * D)
    pieces = [
        [
            returned[g, :, i * WIN + g * W - s : i * WIN + g * W - s + W]
            for g, s in enumerate(starts)
        ]
        for i in range(3)
    ]
    out_w_qkv = jnp.concatenate(pieces[0] + pieces[1] + pieces[2], axis=1)
    out_w_up = jnp.concatenate([returned[g, :, 3 * WIN :] for g in range(F)], axis=1)
    here = rank * rows
    x_own = tokens[0].astype(f32)
    c_own = x_own - jnp.mean(x_own, axis=-1, keepdims=True)
    i_own = lax.rsqrt(jnp.mean(c_own * c_own, axis=-1, keepdims=True) + epsilon)
    n_own = c_own * i_own
    layer_output = (x_own + branch + b_out + b_down).astype(bf16)
    input_grad = cotangent[0].astype(f32) + i_own * (
        mixed_mine
        - jnp.mean(mixed_mine, axis=-1, keepdims=True)
        - n_own * jnp.mean(mixed_mine * n_own, axis=-1, keepdims=True)
    )
    g = [own_small[i * W : (i + 1) * W] for i in range(4)]
    bias_mine = own_small[7 * W : 8 * W]
    return (
        layer_output[None],
        input_grad[None],
        g[0],
        g[1],
        g[2],
        g[3],
        out_w_qkv,
        own_small[4 * W : 7 * W],
        own[:W],
        bias_mine,
        out_w_up,
        own_small[8 * W : 8 * W + FFW],
        own[W : W + FFW],
        bias_mine,
    )


def solution(mesh):
    row = P("fsdp", None)
    vec = P("fsdp")
    act = P("dp", "fsdp", None)
    return jax.shard_map(
        body,
        mesh=mesh,
        in_specs=(act, vec, vec, vec, vec, row, vec, row, vec, row, vec, row, vec, act),
        out_specs=(act, act, vec, vec, vec, vec, row, vec, row, vec, row, vec, row, vec),
        check_vma=False,
    )
```

profile of v0, /device:TPU:0, one launch (start us, length us, event | category | flops | bytes accessed | tf_op | source)
XLA Modules:
  0.0 340.4 jit_solution(5469213770483834597)
XLA Ops:
  8.0 3.0 collective-permute-start
  11.0 3.1 collective-permute-start.1
  14.1 4.8 %concatenate.74 = bf16[12288]{0:T(1024)(128)(2,1)S(1)} concatenate(bf16[96]{0:T(256)(128)(2,1)} %param.15, bf16[96]{0:T(256)(128)(2,1)} %param.16, bf16[96]{0:T(256)(128)(2,1)} %param.17, bf16[96]{0:T(256)(128)(2,1)} %param.18, bf16[96]{0:T(256)(128)(2,1)} %param.22, bf16[96]{0:T(256)(128)(2,1)} %param.26, bf16[288]{0:T(512)(128)(2,1)} %param.20, ...), dimensions={0} | concatenate | bytes 49152 | tf_op jit(solution)/shard_map/concatenate | solution.py:125
  29.4 4.4 %all-to-all-start = ((bf16[8,96,768]{2,1,0:T(8,128)(2,1)}), bf16[8,96,768]{2,1,0:T(8,128)(2,1)}, u32[]{:S(2)}, u32[]{:S(2)}) async-start(bf16[8,96,768]{2,1,0:T(8,128)(2,1)} %fusion.67), calls=%async_computation | async-start | bytes 2359296 | tf_op jit(solution)/shard_map/all_to_all | solution.py:51
  35.0 37.7 %all-gather.8.cloned.1.call-done = bf16[1,1024,768]{2,1,0:T(8,128)(2,1)} async-done(((bf16[1,128,768]{2,1,0:T(8,128)(2,1)}), bf16[1,1024,768]{2,1,0:T(8,128)(2,1)}) %all-gather.8.cloned.1.call-update) | async-done | bytes 1572880 | tf_op jit(solution)/shard_map/all_gather | solution.py:41
  77.3 41.3 %all-gather.6.cloned.1.call-done = bf16[1152,768]{1,0:T(8,128)(2,1)} async-done(((bf16[144,768]{1,0:T(8,128)(2,1)}), bf16[1152,768]{1,0:T(8,128)(2,1)}) %all-gather.6.cloned.1.call-update) | async-done | bytes 1769488 | tf_op jit(solution)/shard_map/all_gather | solution.py:41
  123.4 2.6 add_convert_fusion.4
  126.0 2.4 convolution_add_fusion.1
  132.0 2.4 fusion.69
  134.4 2.4 fusion.29
  136.8 3.3 multiply_convert_fusion
  146.3 2.3 multiply_convert_fusion.1
  150.5 4.1 %fusion.85 = (f32[768]{0:T(1024)S(1)}, f32[768]{0:T(1024)S(1)}, bf16[1024,768]{1,0:T(8,128)(2,1)}, f32[768]{0:T(1024)S(1)}, f32[768]{0:T(1024)S(1)}) fusion(f32[1024]{0:T(1024)S(1)} %get-tuple-element.111, f32[1024]{0:T(1024)S(1)} %get-tuple-element.112, bf16[8,144,768]{2,1,0:T(8,128)(2,1)S(1)} %bitcast.299, f32[768]{0:T(1024)S(1)} %mul.466, ...), kind=kOutput, calls=%fused_computation.216 | convolution fusion | flops 614200320 | bytes 7694336 | tf_op jit(solution)/shard_map/dot_general | solution.py:32
  155.9 4.2 %all-to-all-start.3 = ((f32[8,1,672]{2,1,0:T(1,128)}), f32[8,1,672]{2,1,0:T(1,128)}, u32[]{:S(2)}, u32[]{:S(2)}) async-start(f32[8,1,672]{2,1,0:T(1,128)} %all_to_all.37), calls=%async_computation.3 | async-start | bytes 49152 | tf_op jit(solution)/shard_map/all_to_all | solution.py:46
  160.1 2.6 copy.64
  162.7 3.4 convolution_convert_fusion
  177.4 3.5 %concatenate.91 = bf16[24576]{0:T(1024)(128)(2,1)} concatenate(bf16[672]{0:T(1024)(128)(2,1)} %reduce_sum.192, bf16[96]{0:T(256)(128)(2,1)} %dynamic_slice.41, bf16[384]{0:T(512)(128)(2,1)} %get-tuple-element.123, bf16[23424]{0:T(1024)(128)(2,1)} %broadcast_in_dim.80), dimensions={0} | concatenate | bytes 98304 | tf_op jit(solution)/shard_map/concatenate | solution.py:228
  183.4 27.5 %all_to_all.49 = bf16[4,320,768]{2,1,0:T(8,128)(2,1)} all-to-all(bf16[4,320,768]{2,1,0:T(8,128)(2,1)S(1)} %pad_maximum_fusion), channel_id=1, replica_groups=mesh['dp'=4,'fsdp'=8] {'dp'}, dimensions={0} | all-to-all | bytes 3932160 | tf_op jit(solution)/shard_map/all_to_all | solution.py:62
  213.0 15.6 %all_to_all.50 = bf16[8,24,768]{2,1,0:T(8,128)(2,1)} all-to-all(bf16[8,24,768]{2,1,0:T(8,128)(2,1)S(1)} %bitcast.331), channel_id=1, replica_groups=mesh['dp'=4,'fsdp'=8] {'fsdp'}, dimensions={0} | all-to-all | bytes 589824 | tf_op jit(solution)/shard_map/all_to_all | solution.py:68
  228.6 3.6 %all-to-all-start.2 = ((bf16[8,128,768]{2,1,0:T(8,128)(2,1)}), bf16[8,128,768]{2,1,0:T(8,128)(2,1)S(1)}, u32[]{:S(2)}, u32[]{:S(2)}) async-start(bf16[8,128,768]{2,1,0:T(8,128)(2,1)} %bitcast.326), calls=%async_computation.2 | async-start | bytes 3145728 | tf_op jit(solution)/shard_map/all_to_all | solution.py:46
  233.2 2.7 add_convert_fusion.2
  235.9 32.3 %all-to-all-done.2 = bf16[8,128,768]{2,1,0:T(8,128)(2,1)S(1)} async-done(((bf16[8,128,768]{2,1,0:T(8,128)(2,1)}), bf16[8,128,768]{2,1,0:T(8,128)(2,1)S(1)}, u32[]{:S(2)}, u32[]{:S(2)}) %all-to-all-start.2) | async-done | bytes 1572896 | tf_op jit(solution)/shard_map/all_to_all | solution.py:46
  268.2 4.4 %all-to-all-start.1 = ((bf16[8,128,768]{2,1,0:T(8,128)(2,1)}), bf16[8,128,768]{2,1,0:T(8,128)(2,1)}, u32[]{:S(2)}, u32[]{:S(2)}) async-start(bf16[8,128,768]{2,1,0:T(8,128)(2,1)} %bitcast.313), calls=%async_computation.1 | async-start | bytes 3145728 | tf_op jit(solution)/shard_map/all_to_all | solution.py:46
  274.7 34.3 %all-to-all-done.1 = bf16[8,128,768]{2,1,0:T(8,128)(2,1)} async-done(((bf16[8,128,768]{2,1,0:T(8,128)(2,1)}), bf16[8,128,768]{2,1,0:T(8,128)(2,1)}, u32[]{:S(2)}, u32[]{:S(2)}) %all-to-all-start.1) | async-done | bytes 1572896 | tf_op jit(solution)/shard_map/all_to_all | solution.py:46
  (198 shorter events, 77.9 us)
Async XLA Ops:
  7.2 141.4 %copy-start = (bf16[384,768]{1,0:T(8,128)(2,1)S(1)}, bf16[384,768]{1,0:T(8,128)(2,1)}, u32[]{:S(2)}) copy-start(bf16[384,768]{1,0:T(8,128)(2,1)} %param.25) | copy-start | bytes 1769476
  7.2 65.6 %all-gather.8.cloned.1.call-start = ((), (), s32[]{:S(2)}) async-start(), calls=%async_computation.7 | async-start | bytes 1769472 | tf_op jit(solution)/shard_map/all_gather | solution.py:41
  7.9 110.7 %all-gather.6.cloned.1.call-start = ((), (), s32[]{:S(2)}) async-start(), calls=%async_computation.6 | async-start | bytes 1990656 | tf_op jit(solution)/shard_map/all_gather | solution.py:41
  8.0 67.2 %collective-permute-start = (bf16[96,768]{1,0:T(8,128)(2,1)}, bf16[96,768]{1,0:T(8,128)(2,1)}, u32[]{:S(2)}, u32[]{:S(2)}) collective-permute-start(bf16[96,768]{1,0:T(8,128)(2,1)} %param.21), channel_id=1, source_target_pairs={{0,1},{1,2},{2,3},{3,4},{4,5},{5,6},{6,7},{7,0},{8,9},{9,10},{10,1... | collective-permute-start | bytes 442376 | tf_op jit(solution)/shard_map/ppermute | solution.py:135
  11.0 64.1 %collective-permute-start.1 = (bf16[96,768]{1,0:T(8,128)(2,1)}, bf16[96,768]{1,0:T(8,128)(2,1)}, u32[]{:S(2)}, u32[]{:S(2)}) collective-permute-start(bf16[96,768]{1,0:T(8,128)(2,1)} %param.21), channel_id=1, source_target_pairs={{0,7},{1,0},{2,1},{3,2},{4,3},{5,4},{6,5},{7,6},{8,15},{9,8},{10,9... | collective-permute-start | bytes 442376 | tf_op jit(solution)/shard_map/ppermute | solution.py:136
  20.6 3.0 copy-start.12
  28.0 5.9 %copy-start.18 = (bf16[384]{0:T(512)(128)(2,1)S(1)}, bf16[384]{0:T(512)(128)(2,1)}, u32[]{:S(2)}) copy-start(bf16[384]{0:T(512)(128)(2,1)} %param.24) | copy-start | bytes 2308
  29.4 96.6 %all-to-all-start = ((bf16[8,96,768]{2,1,0:T(8,128)(2,1)}), bf16[8,96,768]{2,1,0:T(8,128)(2,1)}, u32[]{:S(2)}, u32[]{:S(2)}) async-start(bf16[8,96,768]{2,1,0:T(8,128)(2,1)} %fusion.67), calls=%async_computation | async-start | bytes 2359296 | tf_op jit(solution)/shard_map/all_to_all | solution.py:51
  33.8 41.4 %copy-start.14 = (bf16[96,768]{1,0:T(8,128)(2,1)S(1)}, bf16[96,768]{1,0:T(8,128)(2,1)}, u32[]{:S(2)}) copy-start(bf16[96,768]{1,0:T(8,128)(2,1)} %param.21) | copy-start | bytes 442372
  34.0 43.3 %copy-start.19 = (bf16[128]{0:T(256)(128)(2,1)}, bf16[128]{0:T(256)(128)(2,1)S(1)}, u32[]{:S(2)}) copy-start(bf16[128]{0:T(256)(128)(2,1)S(1)} %pad_dynamic-slice_fusion.3) | copy-start | bytes 772
  72.7 2.4 copy-start.2
  118.6 4.2 %copy-start.1 = (bf16[1152,768]{1,0:T(8,128)(2,1)S(1)}, bf16[1152,768]{1,0:T(8,128)(2,1)}, u32[]{:S(2)}) copy-start(bf16[1152,768]{1,0:T(8,128)(2,1)} %all-gather.6.cloned.1.call-done) | copy-start | bytes 5308420
  143.9 2.3 copy-start.6
  150.5 4.1 %copy-start.24 = (bf16[1024,384]{1,0:T(8,128)(2,1)}, bf16[1024,384]{1,0:T(8,128)(2,1)S(1)}, u32[]{:S(2)}) copy-start(bf16[1024,384]{1,0:T(8,128)(2,1)S(1)} %get-tuple-element.124) | copy-start | bytes 2359300
  155.9 19.6 %all-to-all-start.3 = ((f32[8,1,672]{2,1,0:T(1,128)}), f32[8,1,672]{2,1,0:T(1,128)}, u32[]{:S(2)}, u32[]{:S(2)}) async-start(f32[8,1,672]{2,1,0:T(1,128)} %all_to_all.37), calls=%async_computation.3 | async-start | bytes 49152 | tf_op jit(solution)/shard_map/all_to_all | solution.py:46
  175.3 7.2 %copy-start.8 = (bf16[384,768]{1,0:T(8,128)(2,1)S(1)}, bf16[384,768]{1,0:T(8,128)(2,1)}, u32[]{:S(2)}) copy-start(bf16[384,768]{1,0:T(8,128)(2,1)} %fusion.19) | copy-start | bytes 1769476
  213.0 15.6 %copy-start.9 = (bf16[320,768]{1,0:T(8,128)(2,1)}, bf16[320,768]{1,0:T(8,128)(2,1)S(1)}, u32[]{:S(2)}) copy-start(bf16[320,768]{1,0:T(8,128)(2,1)S(1)} %reduce.13) | copy-start | bytes 1474564
  228.6 39.6 %all-to-all-start.2 = ((bf16[8,128,768]{2,1,0:T(8,128)(2,1)}), bf16[8,128,768]{2,1,0:T(8,128)(2,1)S(1)}, u32[]{:S(2)}, u32[]{:S(2)}) async-start(bf16[8,128,768]{2,1,0:T(8,128)(2,1)} %bitcast.326), calls=%async_computation.2 | async-start | bytes 3145728 | tf_op jit(solution)/shard_map/all_to_all | solution.py:46
  268.2 4.5 %slice-start = ((bf16[320,768]{1,0:T(8,128)(2,1)}), bf16[128,768]{1,0:T(8,128)(2,1)S(1)}, s32[]{:S(2)}) async-start(bf16[320,768]{1,0:T(8,128)(2,1)} %copy-done.9), calls=%async_computation.9 | async-start | bytes 393216 | tf_op jit(solution)/shard_map/slice | solution.py:63
  268.2 4.5 %copy-start.10 = (bf16[8,24,768]{2,1,0:T(8,128)(2,1)S(1)}, bf16[8,24,768]{2,1,0:T(8,128)(2,1)}, u32[]{:S(2)}) copy-start(bf16[8,24,768]{2,1,0:T(8,128)(2,1)} %all_to_all.50) | copy-start | bytes 884740
  268.2 40.8 %all-to-all-start.1 = ((bf16[8,128,768]{2,1,0:T(8,128)(2,1)}), bf16[8,128,768]{2,1,0:T(8,128)(2,1)}, u32[]{:S(2)}, u32[]{:S(2)}) async-start(bf16[8,128,768]{2,1,0:T(8,128)(2,1)} %bitcast.313), calls=%async_computation.1 | async-start | bytes 3145728 | tf_op jit(solution)/shard_map/all_to_all | solution.py:46
  272.7 39.0 %all-gather.10.cloned.1.call-start = ((), (), s32[]{:S(2)}) async-start(), calls=%async_computation.8 | async-start | bytes 2457600 | tf_op jit(solution)/shard_map/all_gather | solution.py:70
  274.5 36.2 %copy-start.11 = (bf16[1,128,768]{2,1,0:T(8,128)(2,1)S(1)}, bf16[1,128,768]{2,1,0:T(8,128)(2,1)}, u32[]{:S(2)}) copy-start(bf16[1,128,768]{2,1,0:T(8,128)(2,1)} %param.27) | copy-start | bytes 589828
  316.5 16.8 %copy-start.22 = (f32[96]{0:T(128)}, f32[96]{0:T(128)S(1)}, u32[]{:S(2)}) copy-start(f32[96]{0:T(128)S(1)} %get-tuple-element.176) | copy-start | bytes 1156
  (11 other events, 15.9 us)
Sparse Core Ops, SparseCore 0:
  10.2 62.5 all-gather.7
  75.5 43.0 all-gather.5
  275.6 22.6 all-gather.9
where the time goes:
time: 342 us; the launch traced here: 340 us
  waiting for transfers between devices  146 us (43%)
  local copies, waits for them, and re-layouts  45.6 us (13%)
  blocking collectives  43.1 us (13%)
  matrix products  38.3 us (11%)
  other arithmetic  29.7 us (9%)
  starting transfers between devices  22.9 us (7%)
  between operations  14.6 us (4%)
    all_gather x2, waiting for transfers between devices, gather_rows(): return [lax.all_gather(a, 'fsdp', axis=0, tiled=True) for a in arrays]  79 us
    all_to_all x3, waiting for transfers between devices, scatter_rows(): got = lax.all_to_all(a, 'fsdp', 0, 0, tiled=True)  66.6 us
    all_to_all x1, blocking collectives, return_grads(): lax.all_to_all(both, 'dp', 0, 0, tiled=True).astype(f32)  27.5 us
    dot_general x12, matrix products, dot(): lax.dot_general(a, b, ((dims[0], dims[1]), ((), ())), preferred_element_t...  26.3 us
    all_to_all x1, blocking collectives, return_grads(): part = lax.all_to_all(part, 'fsdp', 0, 0, tiled=True)  15.6 us
    unnamed x72, local copies, waits for them, and re-layouts  14.3 us
    all_to_all x3, starting transfers between devices, scatter_rows(): got = lax.all_to_all(a, 'fsdp', 0, 0, tiled=True)  12.2 us
  transfers between devices with their start and end apart: 9, of which 4 were waited for; matrix products, arithmetic and copies ran while one was open for 15% of the time, Pallas kernels for 0%

commit v1 on v0

--- a/solution.py
+++ b/solution.py
@@ -12,6 +12,28 @@
 inv_root_twopi = 1.0 / math.sqrt(2.0 * math.pi)
 bf16 = jnp.bfloat16
 f32 = jnp.float32
+
+
+def cut_along(shard, dim, length):
+    before, after = (shard.shape[:dim], shard.shape[dim + 1 :])
+    return jnp.moveaxis(shard.reshape(*before, length, -1, *after), dim, 0)
+
+
+def joined_along(tiles, dim):
+    tiles = jnp.moveaxis(tiles, 0, dim)
+    dims = tiles.shape
+    return tiles.reshape(*dims[:dim], dims[dim] * dims[dim + 1], *dims[dim + 2 :])
+
+
+def pairwise_exchange(x, axis, split_dim, concat_dim):
+    peers, place = (lax.axis_size(axis), lax.axis_index(axis))
+    parts = cut_along(x, split_dim, peers)
+    finished = [parts[place]]
+    for step in range(1, peers):
+        sent = parts[place ^ step]
+        finished.append(lax.ppermute(sent, axis, [(i, i ^ step) for i in range(peers)]))
+    parts = jnp.stack(finished)[place ^ jnp.arange(peers)]
+    return joined_along(parts, concat_dim)
 
 
 def rotary(tensor, cosine, sine, direction):
@@ -65,7 +87,7 @@
         part = jnp.sum(lax.all_to_all(parts, "dp", 0, 0, tiled=True).astype(f32), axis=0)
         own_part = jnp.sum(lax.all_to_all(own_parts, "dp", 0, 0, tiled=True).astype(f32), axis=0)
         part, own_part = (part.astype(bf16), own_part.astype(bf16))
-    part = lax.all_to_all(part, "fsdp", 0, 0, tiled=True)
+    part = pairwise_exchange(part, "fsdp", 0, 0)
     if C == D:
         whole = lax.all_gather(jnp.concatenate([part, own_part], axis=0), "dp", axis=0)
         part_all, own_all = (whole[:, : F * (W // n)], whole[:, F * (W // n) :])

time: 342 us -> 318 us (0.930)
  waiting for transfers between devices: 146 us -> 126 us
  starting transfers between devices: 22.9 us -> 39.2 us
  blocking collectives: 43.1 us -> 26.8 us
    all_to_all x3, waiting for transfers between devices: 66.6 us -> 29.2 us  [scatter_rows(): got = lax.all_to_all(a, 'fsdp', 0, 0, tiled=True)]
    ppermute x0 -> x7, waiting for transfers between devices: none -> 16.6 us  [pairwise_exchange(): lax.ppermute(sent, axis, [(i, i ^ step) for i in range(peers)])]
    all_to_all x1 -> x0, blocking collectives: 15.6 us -> none  [return_grads(): part = lax.all_to_all(part, 'fsdp', 0, 0, tiled=True)]
    ppermute x0 -> x7, starting transfers between devices: none -> 15.5 us  [pairwise_exchange(): lax.ppermute(sent, axis, [(i, i ^ step) for i in range(peers)])]
    unnamed x72 -> x96, local copies, waits for them, and re-layouts: 14.3 us -> 9.17 us
    concatenate x1, local copies, waits for them, and re-layouts: 3.53 us -> 0.09 us  [body(): jnp.concatenate([own_small, jnp.zeros(n_small * D - own_small.shape[0], f...]
  transfers between devices with their start and end apart: 9 -> 16, of which waited for: 4 -> 5; matrix products, arithmetic and copies ran while one was open for 15% -> 19% of each run, Pallas kernels for 0% -> 0%
where the time goes in v1:
time: 318 us; the launch traced here: 316 us
  waiting for transfers between devices  126 us (40%)
  local copies, waits for them, and re-layouts  43.4 us (14%)
  matrix products  39.4 us (12%)
  starting transfers between devices  39.2 us (12%)
  other arithmetic  27.3 us (9%)
  blocking collectives  26.8 us (8%)
  between operations  14.7 us (5%)
    all_gather x2, waiting for transfers between devices, gather_rows(): return [lax.all_gather(a, 'fsdp', axis=0, tiled=True) for a in arrays]  79.1 us
    all_to_all x3, waiting for transfers between devices, scatter_rows(): got = lax.all_to_all(a, 'fsdp', 0, 0, tiled=True)  29.2 us
    dot_general x12, matrix products, dot(): lax.dot_general(a, b, ((dims[0], dims[1]), ((), ())), preferred_element_t...  27.5 us
    all_to_all x1, blocking collectives, return_grads(): lax.all_to_all(both, 'dp', 0, 0, tiled=True).astype(f32)  26.8 us
    ppermute x7, waiting for transfers between devices, pairwise_exchange(): lax.ppermute(sent, axis, [(i, i ^ step) for i in range(peers)])  16.6 us
    ppermute x7, starting transfers between devices, pairwise_exchange(): lax.ppermute(sent, axis, [(i, i ^ step) for i in range(peers)])  15.5 us
    all_to_all x3, starting transfers between devices, scatter_rows(): got = lax.all_to_all(a, 'fsdp', 0, 0, tiled=True)  13 us
    unnamed x96, local copies, waits for them, and re-layouts  9.17 us
  transfers between devices with their start and end apart: 16, of which 5 were waited for; matrix products, arithmetic and copies ran while one was open for 19% of the time, Pallas kernels for 0%

profile of v1, /device:TPU:0, one launch (start us, length us, event | category | flops | bytes accessed | tf_op | source)
XLA Modules:
  0.0 316.5 jit_solution(13366992990791433737)
XLA Ops:
  8.0 3.0 collective-permute-start
  11.0 3.1 collective-permute-start.1
  14.1 4.8 %concatenate.74 = bf16[12288]{0:T(1024)(128)(2,1)S(1)} concatenate(bf16[96]{0:T(256)(128)(2,1)} %param.15, bf16[96]{0:T(256)(128)(2,1)} %param.16, bf16[96]{0:T(256)(128)(2,1)} %param.17, bf16[96]{0:T(256)(128)(2,1)} %param.18, bf16[96]{0:T(256)(128)(2,1)} %param.22, bf16[96]{0:T(256)(128)(2,1)} %param.26, bf16[288]{0:T(512)(128)(2,1)} %param.20, ...), dimensions={0} | concatenate | bytes 49152 | tf_op jit(solution)/shard_map/concatenate | solution.py:147
  29.4 4.4 %all-to-all-start = ((bf16[8,96,768]{2,1,0:T(8,128)(2,1)}), bf16[8,96,768]{2,1,0:T(8,128)(2,1)}, u32[]{:S(2)}, u32[]{:S(2)}) async-start(bf16[8,96,768]{2,1,0:T(8,128)(2,1)} %fusion.67), calls=%async_computation | async-start | bytes 2359296 | tf_op jit(solution)/shard_map/all_to_all | solution.py:73
  35.7 37.1 %all-gather.8.cloned.1.call-done = bf16[1,1024,768]{2,1,0:T(8,128)(2,1)} async-done(((bf16[1,128,768]{2,1,0:T(8,128)(2,1)}), bf16[1,1024,768]{2,1,0:T(8,128)(2,1)}) %all-gather.8.cloned.1.call-update) | async-done | bytes 1572880 | tf_op jit(solution)/shard_map/all_gather | solution.py:63
  76.7 42.0 %all-gather.6.cloned.1.call-done = bf16[1152,768]{1,0:T(8,128)(2,1)} async-done(((bf16[144,768]{1,0:T(8,128)(2,1)}), bf16[1152,768]{1,0:T(8,128)(2,1)}) %all-gather.6.cloned.1.call-update) | async-done | bytes 1769488 | tf_op jit(solution)/shard_map/all_gather | solution.py:63
  123.5 2.6 add_convert_fusion.4
  132.1 2.4 fusion.69
  136.9 3.3 %multiply_convert_fusion = bf16[2,1024,1024]{1,2,0:T(8,128)(2,1)S(1)} fusion(f32[2,1024,1024]{1,2,0:T(8,128)S(1)} %get-tuple-element.126, f32[2,1024]{1,0:T(2,128)S(1)} %bitcast.373, f32[2,1024]{1,0:T(2,128)S(1)} %log_add_fusion, pred[1024,1024]{0,1:T(8,128)(4,1)S(1)} %iota_compare_fusion, bf16[1024,2,64]{0,2,1:T(8,128)(2,1)S(1)} %bitcast.372, ...), kind=kOutput, calls=%fused_computation.1 | convolution fusion | flops 278921216 | bytes 14172160 | tf_op jit(solution)/shard_map/qhd,khd->hqk/dot_general | solution.py:212
  151.8 4.1 %fusion.87 = (f32[768]{0:T(1024)S(1)}, f32[768]{0:T(1024)S(1)}, bf16[1024,768]{1,0:T(8,128)(2,1)}, f32[768]{0:T(1024)S(1)}, f32[768]{0:T(1024)S(1)}) fusion(f32[1024]{0:T(1024)S(1)} %get-tuple-element.119, f32[1024]{0:T(1024)S(1)} %get-tuple-element.120, bf16[8,144,768]{2,1,0:T(8,128)(2,1)S(1)} %bitcast.329, f32[768]{0:T(1024)S(1)} %mul.466, ...), kind=kOutput, calls=%fused_computation.236 | convolution fusion | flops 614200320 | bytes 7694336 | tf_op jit(solution)/shard_map/dot_general | solution.py:54
  157.1 3.6 %all-to-all-start.3 = ((f32[8,1,672]{2,1,0:T(1,128)}), f32[8,1,672]{2,1,0:T(1,128)S(1)}, u32[]{:S(2)}, u32[]{:S(2)}) async-start(f32[8,1,672]{2,1,0:T(1,128)} %all_to_all.29), calls=%async_computation.3 | async-start | bytes 49152 | tf_op jit(solution)/shard_map/all_to_all | solution.py:68
  160.7 2.6 copy.64
  163.3 3.4 %convolution_convert_fusion = bf16[8,4,24,384]{3,2,1,0:T(8,128)(2,1)} fusion(bf16[8,4,24,1024]{3,2,1,0:T(8,128)(2,1)} %bitcast.357, bf16[1024,384]{1,0:T(8,128)(2,1)} %copy-done.33), kind=kOutput, calls=%fused_computation.48 | convolution fusion | flops 604274688 | bytes 2949120 | tf_op jit(solution)/shard_map/dot_general | solution.py:54
  176.1 26.8 %all_to_all.37 = bf16[4,320,768]{2,1,0:T(8,128)(2,1)S(1)} all-to-all(bf16[4,320,768]{2,1,0:T(8,128)(2,1)S(1)} %pad_maximum_fusion), channel_id=1, replica_groups=mesh['dp'=4,'fsdp'=8] {'dp'}, dimensions={0} | all-to-all | bytes 3932160 | tf_op jit(solution)/shard_map/all_to_all | solution.py:84
  202.9 5.7 %all-to-all-start.2 = ((bf16[8,128,768]{2,1,0:T(8,128)(2,1)}), bf16[8,128,768]{2,1,0:T(8,128)(2,1)}, u32[]{:S(2)}, u32[]{:S(2)}) async-start(bf16[8,128,768]{2,1,0:T(8,128)(2,1)} %bitcast.355), calls=%async_computation.2 | async-start | bytes 3145728 | tf_op jit(solution)/shard_map/all_to_all | solution.py:68
  208.6 2.6 fusion.96
  214.6 3.8 %add_convert_fusion.2 = bf16[1024,768]{1,0:T(8,128)(2,1)} fusion(f32[1024,768]{1,0:T(8,128)} %fusion.96, bf16[1024,128]{0,1:T(8,128)(2,1)S(1)} %copy-done.9, s32[]{:T(128)S(6)} %select_n.79, bf16[96,768]{1,0:T(8,128)(2,1)} %copy-done.18, bf16[96,768]{1,0:T(8,128)(2,1)S(1)} %copy-done.17, bf16[96,768]{1,0:T(8,128)(2,1)} %copy-done.19, ...), kind=kOutput, calls=%fused_computation.17 | convolution fusion | flops 203685888 | bytes 5423364 | tf_op jit(solution)/shard_map/dot_general | solution.py:54
  219.9 2.9 collective-permute-start.5
  224.3 3.3 %collective-permute-start.7 = (bf16[24,768]{1,0:T(8,128)(2,1)S(1)}, bf16[24,768]{1,0:T(8,128)(2,1)S(1)}, u32[]{:S(2)}, u32[]{:S(2)}) collective-permute-start(bf16[24,768]{1,0:T(8,128)(2,1)S(1)} %get-tuple-element.100), channel_id=1, source_target_pairs={{0,6},{1,7},{2,4},{3,5},{4,2},{5,3},{6,0},{7,1},{8,14},{9,15},{10,... | collective-permute-start | bytes 110600 | tf_op jit(solution)/shard_map/ppermute | solution.py:34
  228.2 8.2 %collective-permute-done.3 = bf16[24,768]{1,0:T(8,128)(2,1)S(1)} collective-permute-done((bf16[24,768]{1,0:T(8,128)(2,1)S(1)}, bf16[24,768]{1,0:T(8,128)(2,1)S(1)}, u32[]{:S(2)}, u32[]{:S(2)}) %collective-permute-start.3) | collective-permute-done | bytes 36896 | tf_op jit(solution)/shard_map/ppermute | solution.py:34
  236.3 4.4 %collective-permute-start.8 = (bf16[24,768]{1,0:T(8,128)(2,1)S(1)}, bf16[24,768]{1,0:T(8,128)(2,1)S(1)}, u32[]{:S(2)}, u32[]{:S(2)}) collective-permute-start(bf16[24,768]{1,0:T(8,128)(2,1)S(1)} %get-tuple-element.99), channel_id=1, source_target_pairs={{0,7},{1,6},{2,5},{3,4},{4,3},{5,2},{6,1},{7,0},{8,15},{9,14},{10,... | collective-permute-start | bytes 110600 | tf_op jit(solution)/shard_map/ppermute | solution.py:34
  241.9 8.4 %collective-permute-done.5 = bf16[24,768]{1,0:T(8,128)(2,1)S(1)} collective-permute-done((bf16[24,768]{1,0:T(8,128)(2,1)S(1)}, bf16[24,768]{1,0:T(8,128)(2,1)S(1)}, u32[]{:S(2)}, u32[]{:S(2)}) %collective-permute-start.5) | collective-permute-done | bytes 36896 | tf_op jit(solution)/shard_map/ppermute | solution.py:34
  251.0 3.7 %all-to-all-start.1 = ((bf16[8,128,768]{2,1,0:T(8,128)(2,1)}), bf16[8,128,768]{2,1,0:T(8,128)(2,1)S(1)}, u32[]{:S(2)}, u32[]{:S(2)}) async-start(bf16[8,128,768]{2,1,0:T(8,128)(2,1)} %bitcast.20), calls=%async_computation.1 | async-start | bytes 3145728 | tf_op jit(solution)/shard_map/all_to_all | solution.py:68
  261.6 29.2 %all-to-all-done.1 = bf16[8,128,768]{2,1,0:T(8,128)(2,1)S(1)} async-done(((bf16[8,128,768]{2,1,0:T(8,128)(2,1)}), bf16[8,128,768]{2,1,0:T(8,128)(2,1)S(1)}, u32[]{:S(2)}, u32[]{:S(2)}) %all-to-all-start.1) | async-done | bytes 1572896 | tf_op jit(solution)/shard_map/all_to_all | solution.py:68
  (240 shorter events, 86.4 us)
Async XLA Ops:
  7.2 142.6 %copy-start = (bf16[384,768]{1,0:T(8,128)(2,1)S(1)}, bf16[384,768]{1,0:T(8,128)(2,1)}, u32[]{:S(2)}) copy-start(bf16[384,768]{1,0:T(8,128)(2,1)} %param.25) | copy-start | bytes 1769476
  7.2 65.6 %all-gather.8.cloned.1.call-start = ((), (), s32[]{:S(2)}) async-start(), calls=%async_computation.6 | async-start | bytes 1769472 | tf_op jit(solution)/shard_map/all_gather | solution.py:63
  7.9 110.7 %all-gather.6.cloned.1.call-start = ((), (), s32[]{:S(2)}) async-start(), calls=%async_computation.5 | async-start | bytes 1990656 | tf_op jit(solution)/shard_map/all_gather | solution.py:63
  8.0 67.2 %collective-permute-start = (bf16[96,768]{1,0:T(8,128)(2,1)}, bf16[96,768]{1,0:T(8,128)(2,1)S(1)}, u32[]{:S(2)}, u32[]{:S(2)}) collective-permute-start(bf16[96,768]{1,0:T(8,128)(2,1)} %param.21), channel_id=1, source_target_pairs={{0,1},{1,2},{2,3},{3,4},{4,5},{5,6},{6,7},{7,0},{8,9},{9,10},{10,1... | collective-permute-start | bytes 442376 | tf_op jit(solution)/shard_map/ppermute | solution.py:157
  11.0 64.2 %collective-permute-start.1 = (bf16[96,768]{1,0:T(8,128)(2,1)}, bf16[96,768]{1,0:T(8,128)(2,1)S(1)}, u32[]{:S(2)}, u32[]{:S(2)}) collective-permute-start(bf16[96,768]{1,0:T(8,128)(2,1)} %param.21), channel_id=1, source_target_pairs={{0,7},{1,0},{2,1},{3,2},{4,3},{5,4},{6,5},{7,6},{8,15},{9,8},{10,9... | collective-permute-start | bytes 442376 | tf_op jit(solution)/shard_map/ppermute | solution.py:158
  28.0 5.9 %copy-start.26 = (bf16[384]{0:T(512)(128)(2,1)S(1)}, bf16[384]{0:T(512)(128)(2,1)}, u32[]{:S(2)}) copy-start(bf16[384]{0:T(512)(128)(2,1)} %param.24) | copy-start | bytes 2308
  29.4 96.7 %all-to-all-start = ((bf16[8,96,768]{2,1,0:T(8,128)(2,1)}), bf16[8,96,768]{2,1,0:T(8,128)(2,1)}, u32[]{:S(2)}, u32[]{:S(2)}) async-start(bf16[8,96,768]{2,1,0:T(8,128)(2,1)} %fusion.67), calls=%async_computation | async-start | bytes 2359296 | tf_op jit(solution)/shard_map/all_to_all | solution.py:73
  33.9 41.3 %copy-start.16 = (bf16[96,768]{1,0:T(8,128)(2,1)S(1)}, bf16[96,768]{1,0:T(8,128)(2,1)}, u32[]{:S(2)}) copy-start(bf16[96,768]{1,0:T(8,128)(2,1)} %param.21) | copy-start | bytes 442372
  34.6 42.0 %copy-start.27 = (bf16[128]{0:T(256)(128)(2,1)}, bf16[128]{0:T(256)(128)(2,1)S(1)}, u32[]{:S(2)}) copy-start(bf16[128]{0:T(256)(128)(2,1)S(1)} %pad_dynamic-slice_fusion.3) | copy-start | bytes 772
  157.1 18.1 %all-to-all-start.3 = ((f32[8,1,672]{2,1,0:T(1,128)}), f32[8,1,672]{2,1,0:T(1,128)S(1)}, u32[]{:S(2)}, u32[]{:S(2)}) async-start(f32[8,1,672]{2,1,0:T(1,128)} %all_to_all.29), calls=%async_computation.3 | async-start | bytes 49152 | tf_op jit(solution)/shard_map/all_to_all | solution.py:68
  202.9 48.1 %all-to-all-start.2 = ((bf16[8,128,768]{2,1,0:T(8,128)(2,1)}), bf16[8,128,768]{2,1,0:T(8,128)(2,1)}, u32[]{:S(2)}, u32[]{:S(2)}) async-start(bf16[8,128,768]{2,1,0:T(8,128)(2,1)} %bitcast.355), calls=%async_computation.2 | async-start | bytes 3145728 | tf_op jit(solution)/shard_map/all_to_all | solution.py:68
  211.8 6.6 %copy-start.10 = (bf16[320,768]{1,0:T(8,128)(2,1)}, bf16[320,768]{1,0:T(8,128)(2,1)S(1)}, u32[]{:S(2)}) copy-start(bf16[320,768]{1,0:T(8,128)(2,1)S(1)} %reduce.13) | copy-start | bytes 1474564
  212.6 11.7 %collective-permute-start.2 = (bf16[24,768]{1,0:T(8,128)(2,1)S(1)}, bf16[24,768]{1,0:T(8,128)(2,1)S(1)}, u32[]{:S(2)}, u32[]{:S(2)}) collective-permute-start(bf16[24,768]{1,0:T(8,128)(2,1)S(1)} %get-tuple-element.105), channel_id=1, source_target_pairs={{0,1},{1,0},{2,3},{3,2},{4,5},{5,4},{6,7},{7,6},{8,9},{9,8},{10,11... | collective-permute-start | bytes 110600 | tf_op jit(solution)/shard_map/ppermute | solution.py:34
  218.4 17.9 %collective-permute-start.3 = (bf16[24,768]{1,0:T(8,128)(2,1)S(1)}, bf16[24,768]{1,0:T(8,128)(2,1)S(1)}, u32[]{:S(2)}, u32[]{:S(2)}) collective-permute-start(bf16[24,768]{1,0:T(8,128)(2,1)S(1)} %get-tuple-element.104), channel_id=1, source_target_pairs={{0,2},{1,3},{2,0},{3,1},{4,6},{5,7},{6,4},{7,5},{8,10},{9,11},{10,... | collective-permute-start | bytes 110600 | tf_op jit(solution)/shard_map/ppermute | solution.py:34
  219.9 21.4 %collective-permute-start.4 = (bf16[24,768]{1,0:T(8,128)(2,1)S(1)}, bf16[24,768]{1,0:T(8,128)(2,1)S(1)}, u32[]{:S(2)}, u32[]{:S(2)}) collective-permute-start(bf16[24,768]{1,0:T(8,128)(2,1)S(1)} %get-tuple-element.103), channel_id=1, source_target_pairs={{0,3},{1,2},{2,1},{3,0},{4,7},{5,6},{6,5},{7,4},{8,11},{9,10},{10,... | collective-permute-start | bytes 110600 | tf_op jit(solution)/shard_map/ppermute | solution.py:34
  219.9 30.5 %collective-permute-start.5 = (bf16[24,768]{1,0:T(8,128)(2,1)S(1)}, bf16[24,768]{1,0:T(8,128)(2,1)S(1)}, u32[]{:S(2)}, u32[]{:S(2)}) collective-permute-start(bf16[24,768]{1,0:T(8,128)(2,1)S(1)} %get-tuple-element.102), channel_id=1, source_target_pairs={{0,4},{1,5},{2,6},{3,7},{4,0},{5,1},{6,2},{7,3},{8,12},{9,13},{10,... | collective-permute-start | bytes 110600 | tf_op jit(solution)/shard_map/ppermute | solution.py:34
  222.8 32.0 %collective-permute-start.6 = (bf16[24,768]{1,0:T(8,128)(2,1)}, bf16[24,768]{1,0:T(8,128)(2,1)S(1)}, u32[]{:S(2)}, u32[]{:S(2)}) collective-permute-start(bf16[24,768]{1,0:T(8,128)(2,1)} %get-tuple-element.101), channel_id=1, source_target_pairs={{0,5},{1,4},{2,7},{3,6},{4,1},{5,0},{6,3},{7,2},{8,13},{9,12},{10,... | collective-permute-start | bytes 110600 | tf_op jit(solution)/shard_map/ppermute | solution.py:34
  224.3 31.1 %collective-permute-start.7 = (bf16[24,768]{1,0:T(8,128)(2,1)S(1)}, bf16[24,768]{1,0:T(8,128)(2,1)S(1)}, u32[]{:S(2)}, u32[]{:S(2)}) collective-permute-start(bf16[24,768]{1,0:T(8,128)(2,1)S(1)} %get-tuple-element.100), channel_id=1, source_target_pairs={{0,6},{1,7},{2,4},{3,5},{4,2},{5,3},{6,0},{7,1},{8,14},{9,15},{10,... | collective-permute-start | bytes 110600 | tf_op jit(solution)/shard_map/ppermute | solution.py:34
  236.3 19.7 %collective-permute-start.8 = (bf16[24,768]{1,0:T(8,128)(2,1)S(1)}, bf16[24,768]{1,0:T(8,128)(2,1)S(1)}, u32[]{:S(2)}, u32[]{:S(2)}) collective-permute-start(bf16[24,768]{1,0:T(8,128)(2,1)S(1)} %get-tuple-element.99), channel_id=1, source_target_pairs={{0,7},{1,6},{2,5},{3,4},{4,3},{5,2},{6,1},{7,0},{8,15},{9,14},{10,... | collective-permute-start | bytes 110600 | tf_op jit(solution)/shard_map/ppermute | solution.py:34
  251.0 7.2 %slice-start = ((bf16[320,768]{1,0:T(8,128)(2,1)}), bf16[128,768]{1,0:T(8,128)(2,1)S(1)}, s32[]{:S(2)}) async-start(bf16[320,768]{1,0:T(8,128)(2,1)} %copy-done.10), calls=%async_computation.8 | async-start | bytes 393216 | tf_op jit(solution)/shard_map/slice | solution.py:85
  251.0 39.8 %all-to-all-start.1 = ((bf16[8,128,768]{2,1,0:T(8,128)(2,1)}), bf16[8,128,768]{2,1,0:T(8,128)(2,1)S(1)}, u32[]{:S(2)}, u32[]{:S(2)}) async-start(bf16[8,128,768]{2,1,0:T(8,128)(2,1)} %bitcast.20), calls=%async_computation.1 | async-start | bytes 3145728 | tf_op jit(solution)/shard_map/all_to_all | solution.py:68
  254.7 37.3 %all-gather.10.cloned.1.call-start = ((), (), s32[]{:S(2)}) async-start(), calls=%async_computation.7 | async-start | bytes 2457600 | tf_op jit(solution)/shard_map/all_gather | solution.py:92
  261.4 29.7 %copy-start.11 = (bf16[1,128,768]{2,1,0:T(8,128)(2,1)S(1)}, bf16[1,128,768]{2,1,0:T(8,128)(2,1)}, u32[]{:S(2)}) copy-start(bf16[1,128,768]{2,1,0:T(8,128)(2,1)} %param.27) | copy-start | bytes 589828
  299.4 10.1 %copy-start.31 = (f32[96]{0:T(128)}, f32[96]{0:T(128)S(1)}, u32[]{:S(2)}) copy-start(f32[96]{0:T(128)S(1)} %get-tuple-element.184) | copy-start | bytes 1156
  (27 other events, 59.0 us)
Sparse Core Ops, SparseCore 0:
  10.2 62.5 all-gather.7
  75.5 43.0 all-gather.5
  259.1 22.4 all-gather.9
